TPU v7x, 32 devices: a whole 2x2x4 slice. The times are simulated.
32 devices in a mesh: lat: 16 (over z, y, x), field: 2 (over core).
Axes of the slice: x: 2, y: 2, z: 4, core: 2. Of those that a mesh axis runs over, the one named last changes fastest.
Arguments:
- fields_grid: bfloat16 [2, 64, 2, 48, 192], P('field', None, None, 'lat'), may hold values from -6 to 6
- basis: bfloat16 [128, 48, 96], P('lat'), may hold values from -0.875 to 0.875
- order_table: int32 [16, 8], replicated, may hold values from -1 to 95, as said below
- panel_modes: int32 [2, 64], replicated, may hold values from 0 to 95, as said below
Outputs:
- panel: bfloat16 [2, 128, 192, 128], P('field', 'lat')
Inputs may be any that keep to these rules, and one draw needn't show every extreme that they name: `order_table`: each order 0 to 95 stands in exactly one slot; every other slot holds -1; some group has all 8 slots filled. `panel_modes`: row 1 is never smaller than row 0 in the same column; degree 95 appears.
All inputs are finite; a program needn't handle non-finite values.
Results may differ from a plain program's by a relative error of at most 0.0082.
Values may be sent and summed in bfloat16 or wider, within the bound.
A program may use at most 64 MiB of HBM per device.

v0:
```python
import math
import jax
import jax.numpy as jnp
from jax import lax
from jax.sharding import PartitionSpec as P


def dft_table(orders, lon_count):
    valid_slot = orders >= 0
    safe_orders = jnp.maximum(orders, 0)
    products = lax.broadcasted_iota(jnp.int32, (lon_count, 1), 0) * safe_orders[None, :] % lon_count
    angles = products.astype(jnp.float32) * (2.0 * math.pi / lon_count)
    cosine = jnp.where(valid_slot[None, :], jnp.cos(angles), 0.0).astype(jnp.bfloat16)
    sine_table = jnp.where(valid_slot[None, :], -jnp.sin(angles), 0.0).astype(jnp.bfloat16)
    return jnp.stack([cosine, sine_table], axis=1)


def local(fields_grid, basis, order_table, panel_modes):
    grid_one = fields_grid[0]
    snap_count = grid_one.shape[0]
    pair_count = grid_one.shape[2]
    lon_count = grid_one.shape[3]
    slot_count = order_table.shape[1]
    deg_count = basis.shape[2]
    pair_total = basis.shape[1]
    mode_count = panel_modes.shape[1]
    orders = order_table.reshape(-1)
    slot_all = orders.shape[0]
    dft = dft_table(orders, lon_count)
    fourier = jnp.einsum("thjn,nrk->hkjrt", grid_one, dft, preferred_element_type=jnp.float32) * (
        1.0 / math.sqrt(lon_count)
    )
    fourier = fourier.reshape(2, slot_all, pair_count, 2 * snap_count)
    parity_parts = jnp.stack([fourier[0] + fourier[1], fourier[0] - fourier[1]]).astype(
        jnp.bfloat16
    )
    group_index = lax.axis_index("lat")
    my_orders = lax.dynamic_slice_in_dim(order_table, group_index, 1, 0)[0]
    my_odd = my_orders % 2 == 1
    basis_split = basis.reshape(slot_count, pair_total, deg_count // 2, 2)
    even_rows = basis_split[:, :, :, 0]
    odd_rows = basis_split[:, :, :, 1]
    degree = lax.broadcasted_iota(jnp.int32, (1, deg_count), 1)
    keep_mask = (degree >= my_orders[:, None]) & (my_orders >= 0)[:, None]
    received = lax.all_to_all(parity_parts, "lat", split_axis=1, concat_axis=2, tiled=True)
    first_parity = jnp.where(my_odd[:, None, None], received[1], received[0])
    second = jnp.where(my_odd[:, None, None], received[0], received[1])
    low_degrees = jnp.einsum(
        "sjh,sjc->shc", even_rows, first_parity, preferred_element_type=jnp.float32
    )
    high_degrees = jnp.einsum("sjh,sjc->shc", odd_rows, second, preferred_element_type=jnp.float32)
    joined = jnp.stack([low_degrees, high_degrees], axis=2).reshape(slot_count, deg_count, -1)
    coefficients = jnp.where(keep_mask[:, :, None], joined, 0.0).astype(jnp.bfloat16)
    mode_order = panel_modes[0]
    mode_degree = panel_modes[1]
    onehot = (my_orders[None, :] == mode_order[:, None]).astype(jnp.bfloat16)
    picked = jnp.take(coefficients, mode_degree, axis=1)
    local_values = jnp.einsum("ms,smc->mc", onehot, picked, preferred_element_type=jnp.float32)
    field_index = lax.axis_index("field")
    both_fields = jnp.stack(
        [
            jnp.where(field_index == 0, local_values, 0.0),
            jnp.where(field_index == 1, local_values, 0.0),
        ]
    )
    summed = lax.psum(both_fields, ("lat", "field"))
    other_field = jnp.where(field_index == 0, summed[1], summed[0]).astype(jnp.bfloat16)
    columns = other_field.astype(jnp.float32).reshape(mode_count * 2, snap_count)
    centered = (columns - jnp.mean(columns, axis=1, keepdims=True)).astype(jnp.bfloat16)
    coef_rows = coefficients.reshape(slot_count * deg_count * 2, snap_count)
    panel_values = lax.dot_general(
        coef_rows, centered, (((1,), (1,)), ((), ())), preferred_element_type=jnp.float32
    )
    panel_values = panel_values * (1.0 / (snap_count - 1))
    return panel_values.astype(jnp.bfloat16).reshape(1, slot_count, 2 * deg_count, 2 * mode_count)


def solution(mesh):
    placed = (P("field", None, None, "lat", None), P("lat", None, None), P(), P())
    return jax.shard_map(
        local, mesh=mesh, in_specs=placed, out_specs=P("field", "lat", None, None), check_vma=False
    )
```

profile of v0, /device:TPU:0, one launch (start us, length us, event | category | flops | bytes accessed | tf_op | source)
XLA Modules:
  0.0 63.5 jit_solution(17050038539362757233)
XLA Ops:
  0.0 0.0 copy-start.1
  0.0 0.8 %broadcast_compare_fusion = pred[16,8]{0,1:T(8,128)(4,1)S(1)} fusion(s32[16,8]{0,1:T(8,128)} %param.6), kind=kLoop, calls=%fused_computation.57 | loop fusion | flops 128 | bytes 640 | tf_op jit(solution)/shard_map/ge | solution.py:9
  0.8 0.0 copy-done.1
  0.8 0.1 copy.39
  0.9 0.1 ge.51
  1.0 0.1 copy.40
  1.0 0.1 max.11
  1.1 0.4 select_convert_fusion.1
  1.6 1.1 %fusion.1 = f32[2,128,3,2,64]{1,4,2,0,3:T(8,128)S(1)} fusion(bf16[64,2,3,192]{3,1,2,0:T(2,128)(2,1)} %bitcast.69, bf16[192,1,128]{2,0,1:T(8,128)(2,1)S(1)} %get-tuple-element.16, bf16[192,1,128]{2,0,1:T(8,128)(2,1)S(1)} %get-tuple-element.15), kind=kOutput, calls=%fused_computation.4 | convolution fusion | flops 38043648 | bytes 638976 | tf_op jit(solution)/shard_map/thjn,nrk->hkjrt/dot_general | solution.py:30
  2.8 0.8 %copy.44 = bf16[2,128,3,128]{3,0,2,1:T(2,128)(2,1)} copy(bf16[2,128,3,128]{1,3,2,0:T(8,128)(2,1)S(1)} %pad_maximum_fusion.1) | data formatting | bytes 393216 | tf_op jit(solution)/shard_map/stack | solution.py:34
  3.7 0.0 copy-start
  3.7 8.5 %all-to-all-start = ((bf16[2,128,3,128]{3,0,2,1:T(2,128)(2,1)}), bf16[2,128,3,128]{3,0,2,1:T(2,128)(2,1)S(1)}, u32[]{:S(2)}, u32[]{:S(2)}) async-start(bf16[2,128,3,128]{3,0,2,1:T(2,128)(2,1)} %copy.44), calls=%async_computation | async-start | bytes 393216 | tf_op jit(solution)/shard_map/all_to_all | solution.py:45
  12.1 0.0 copy-start.2
  12.2 0.7 %copy-done.2 = s32[2,64]{1,0:T(2,128)S(1)} copy-done((s32[2,64]{1,0:T(2,128)S(1)}, s32[2,64]{1,0:T(2,128)}, u32[]{:S(2)}) %copy-start.2) | copy-done | bytes 536
  12.8 0.2 dynamic-slice_reduce_fusion
  13.0 0.1 compare_bitcast_fusion
  13.2 0.0 copy-done
  13.2 0.2 copy.48
  13.4 7.4 %all-to-all-done = bf16[2,128,3,128]{3,0,2,1:T(2,128)(2,1)S(1)} async-done(((bf16[2,128,3,128]{3,0,2,1:T(2,128)(2,1)}), bf16[2,128,3,128]{3,0,2,1:T(2,128)(2,1)S(1)}, u32[]{:S(2)}, u32[]{:S(2)}) %all-to-all-start) | async-done | bytes 196640 | tf_op jit(solution)/shard_map/all_to_all | solution.py:45
  20.9 0.1 bitcast_select_fusion.2
  21.0 0.2 convolution_bitcast_fusion.1
  21.2 0.2 convolution_bitcast_fusion
  21.4 0.1 copy.53
  21.5 0.2 fusion.2
  21.7 0.6 gather_fusion
  22.3 0.3 fusion.5
  22.6 39.0 %psum.7 = bf16[2,64,128]{2,1,0:T(8,128)(2,1)S(1)} all-reduce(f32[2,64,128]{2,1,0:T(8,128)S(1)} %pad_maximum_fusion.2), channel_id=1, replica_groups=mesh['lat'=16,'field'=2] {'lat','field'}, use_global_device_ids=true, to_apply=%region_0.1 | all-reduce | flops 16384 | bytes 98304 | tf_op jit(solution)/shard_map/psum | solution.py:66
  61.6 0.1 reshape.345
  61.7 0.1 reduce_sum.9
  61.8 0.1 div.10
  62.0 0.1 sub.26
  62.1 0.1 sub.27
  62.2 0.1 convert_element_type.92
  62.3 0.2 convert_element_type.86
  62.5 1.0 %fusion = bf16[1536,128]{1,0:T(8,128)(2,1)} fusion(bf16[1536,64]{1,0:T(8,128)(2,1)S(1)} %convert_element_type.86, bf16[128,64]{1,0:T(8,128)(2,1)S(1)} %convert_element_type.92), kind=kOutput, calls=%fused_computation.2 | convolution fusion | flops 25559040 | bytes 606208 | tf_op jit(solution)/shard_map/dot_general | solution.py:71
  (23 shorter events, 0.3 us)
Async XLA Ops:
  0.0 0.8 %copy-start.1 = (s32[16,8]{0,1:T(8,128)S(1)}, s32[16,8]{0,1:T(8,128)}, u32[]{:S(2)}) copy-start(s32[16,8]{0,1:T(8,128)} %param.6) | copy-start | bytes 1540
  3.7 9.5 %copy-start = (bf16[8,48,96]{2,1,0:T(8,128)(2,1)S(1)}, bf16[8,48,96]{2,1,0:T(8,128)(2,1)}, u32[]{:S(2)}) copy-start(bf16[8,48,96]{2,1,0:T(8,128)(2,1)} %param.5) | copy-start | bytes 221188
  3.7 17.1 %all-to-all-start = ((bf16[2,128,3,128]{3,0,2,1:T(2,128)(2,1)}), bf16[2,128,3,128]{3,0,2,1:T(2,128)(2,1)S(1)}, u32[]{:S(2)}, u32[]{:S(2)}) async-start(bf16[2,128,3,128]{3,0,2,1:T(2,128)(2,1)} %copy.44), calls=%async_computation | async-start | bytes 393216 | tf_op jit(solution)/shard_map/all_to_all | solution.py:45
  12.1 0.7 %copy-start.2 = (s32[2,64]{1,0:T(2,128)S(1)}, s32[2,64]{1,0:T(2,128)}, u32[]{:S(2)}) copy-start(s32[2,64]{1,0:T(2,128)} %param.7) | copy-start | bytes 1540
where the time goes:
time: 63.9 us; the launch traced here: 63.5 us
  blocking collectives  39 us (61%)
  starting transfers between devices  8.47 us (13%)
  waiting for transfers between devices  7.41 us (12%)
  local copies, waits for them, and re-layouts  3.74 us (6%)
  matrix products  2.79 us (4%)
  other arithmetic  1.84 us (3%)
    psum x1, blocking collectives, local(): summed = lax.psum(both_fields, ('lat', 'field'))  39 us
    all_to_all x1, starting transfers between devices, local(): lax.all_to_all(parity_parts, 'lat', split_axis=1, concat_axis=2, tiled=True)  8.47 us
    all_to_all x1, waiting for transfers between devices, local(): lax.all_to_all(parity_parts, 'lat', split_axis=1, concat_axis=2, tiled=True)  7.41 us
  transfers between devices with their start and end apart: 1, of which 1 were waited for; matrix products, arithmetic and copies ran while one was open for 1% of the time, Pallas kernels for 0%

commit v1 on v0

--- a/solution.py
+++ b/solution.py
@@ -42,7 +42,12 @@
     odd_rows = basis_split[:, :, :, 1]
     degree = lax.broadcasted_iota(jnp.int32, (1, deg_count), 1)
     keep_mask = (degree >= my_orders[:, None]) & (my_orders >= 0)[:, None]
-    received = lax.all_to_all(parity_parts, "lat", split_axis=1, concat_axis=2, tiled=True)
+    received = jnp.concatenate(
+        lax.all_to_all(
+            jnp.stack(jnp.split(parity_parts, lax.axis_size("lat"), axis=1)), "lat", 0, 0
+        ),
+        axis=2,
+    )
     first_parity = jnp.where(my_odd[:, None, None], received[1], received[0])
     second = jnp.where(my_odd[:, None, None], received[0], received[1])
     low_degrees = jnp.einsum(

time: 63.9 us -> 75.6 us (1.18)
  local copies, waits for them, and re-layouts: 3.74 us -> 14.4 us
  other arithmetic: 1.84 us -> 2.84 us
    unnamed x7 -> x22, local copies, waits for them, and re-layouts: 0.84 us -> 9.9 us
    another operation x3 -> x19, local copies, waits for them, and re-layouts: 0.86 us -> 2.54 us  [the longest x17 2.53 us: local(): jnp.stack(jnp.split(parity_parts, lax.axis_size('lat'), axis=1))]
    another operation x2 -> x3, other arithmetic: 0.06 us -> 1.07 us  [the longest x2 1.03 us: local(): jnp.stack(jnp.split(parity_parts, lax.axis_size('lat'), axis=1))]
    max x1, other arithmetic: 0.01 us -> 0.76 us  [dft_table(): safe_orders = jnp.maximum(orders, 0)]
    ge x1, other arithmetic: 0.76 us -> 0.01 us  [dft_table(): valid_slot = orders >= 0]
where the time goes in v1:
time: 75.6 us; the launch traced here: 75.2 us
  blocking collectives  39 us (52%)
  local copies, waits for them, and re-layouts  14.4 us (19%)
  starting transfers between devices  8.47 us (11%)
  waiting for transfers between devices  7.42 us (10%)
  other arithmetic  2.84 us (4%)
  matrix products  2.79 us (4%)
    psum x1, blocking collectives, local(): summed = lax.psum(both_fields, ('lat', 'field'))  39 us
    unnamed x22, local copies, waits for them, and re-layouts  9.9 us
    all_to_all x1, starting transfers between devices, local(): lax.all_to_all(jnp.stack(jnp.split(parity_parts, lax.axis_size('lat'), ax...  8.47 us
    all_to_all x1, waiting for transfers between devices, local(): lax.all_to_all(jnp.stack(jnp.split(parity_parts, lax.axis_size('lat'), ax...  7.42 us
    another operation x17, local copies, waits for them, and re-layouts, local(): jnp.stack(jnp.split(parity_parts, lax.axis_size('lat'), axis=1))  2.53 us
  transfers between devices with their start and end apart: 1, of which 1 were waited for; matrix products, arithmetic and copies ran while one was open for 1% of the time, Pallas kernels for 0%

profile of v1, /device:TPU:0, one launch (start us, length us, event | category | flops | bytes accessed | tf_op | source)
XLA Modules:
  0.0 75.2 jit_solution(9530882271355810809)
XLA Ops:
  0.0 0.8 %broadcast_maximum_fusion = s32[16,8]{0,1:T(8,128)S(1)} fusion(s32[16,8]{0,1:T(8,128)} %param.6), kind=kLoop, calls=%fused_computation.133 | loop fusion | flops 128 | bytes 1024 | tf_op jit(solution)/shard_map/max | solution.py:10
  0.8 0.1 copy.38
  0.8 0.1 max.11
  0.9 0.1 copy.37
  1.0 0.1 ge.51
  1.1 0.4 select_convert_fusion.1
  1.6 1.1 %fusion.1 = f32[2,128,3,2,64]{1,4,2,0,3:T(8,128)S(1)} fusion(bf16[64,2,3,192]{3,1,2,0:T(2,128)(2,1)} %bitcast.101, bf16[192,1,128]{2,0,1:T(8,128)(2,1)S(1)} %get-tuple-element.32, bf16[192,1,128]{2,0,1:T(8,128)(2,1)S(1)} %get-tuple-element.31), kind=kOutput, calls=%fused_computation.4 | convolution fusion | flops 38043648 | bytes 638976 | tf_op jit(solution)/shard_map/thjn,nrk->hkjrt/dot_general | solution.py:30
  2.8 0.6 fusion.33
  3.4 0.4 fusion.4
  3.8 0.1 copy.42
  3.9 0.6 constant_dynamic-update-slice_fusion.15
  4.6 0.1 copy.43
  4.7 0.1 copy.44
  4.8 0.1 copy.45
  4.9 0.1 copy.46
  5.0 0.1 copy.47
  5.2 0.1 copy.48
  5.3 0.1 copy.49
  5.4 0.1 copy.50
  5.5 0.1 copy.51
  5.6 0.1 copy.52
  5.8 0.1 copy.53
  5.9 0.1 copy.54
  6.0 0.1 copy.55
  6.1 0.1 copy.56
  6.3 0.1 copy.57
  6.4 0.6 constant_dynamic-update-slice_fusion.14
  7.0 0.6 constant_dynamic-update-slice_fusion.13
  7.6 0.6 constant_dynamic-update-slice_fusion.12
  8.2 0.6 constant_dynamic-update-slice_fusion.11
  8.8 0.6 constant_dynamic-update-slice_fusion.10
  9.4 0.6 constant_dynamic-update-slice_fusion.9
  10.0 0.6 constant_dynamic-update-slice_fusion.8
  10.6 0.6 constant_dynamic-update-slice_fusion.7
  11.2 0.6 constant_dynamic-update-slice_fusion.6
  11.8 0.6 constant_dynamic-update-slice_fusion.5
  12.4 0.6 constant_dynamic-update-slice_fusion.4
  13.0 0.6 constant_dynamic-update-slice_fusion.3
  13.6 0.6 constant_dynamic-update-slice_fusion.2
  14.2 0.6 constant_dynamic-update-slice_fusion.1
  14.8 0.6 constant_dynamic-update-slice_fusion
  15.4 8.5 %all-to-all-start = ((bf16[16,2,8,3,128]{4,2,3,1,0:T(8,128)(2,1)}), bf16[16,2,8,3,128]{4,2,3,1,0:T(8,128)(2,1)S(1)}, u32[]{:S(2)}, u32[]{:S(2)}) async-start(bf16[16,2,8,3,128]{4,2,3,1,0:T(8,128)(2,1)} %constant_dynamic-update-slice_fusion), calls=%async_computation | async-start | bytes 393216 | tf_op jit(solution)/shard_map/all_to_all | solution.py:46
  23.9 0.0 copy-start.2
  23.9 0.7 copy-done.2
  24.6 0.2 dynamic-slice_reduce_fusion
  24.8 0.1 compare_bitcast_fusion
  24.9 0.2 copy.59
  25.1 7.4 %all-to-all-done = bf16[16,2,8,3,128]{4,2,3,1,0:T(8,128)(2,1)S(1)} async-done(((bf16[16,2,8,3,128]{4,2,3,1,0:T(8,128)(2,1)}), bf16[16,2,8,3,128]{4,2,3,1,0:T(8,128)(2,1)S(1)}, u32[]{:S(2)}, u32[]{:S(2)}) %all-to-all-start) | async-done | bytes 196640 | tf_op jit(solution)/shard_map/all_to_all | solution.py:46
  32.6 0.1 bitcast_select_fusion.2
  32.7 0.2 convolution_bitcast_fusion.1
  32.9 0.2 convolution_bitcast_fusion
  33.1 0.1 copy.64
  33.2 0.2 fusion.2
  33.4 0.6 gather_fusion
  34.0 0.3 fusion.36
  34.3 39.0 %psum.7 = bf16[2,64,128]{2,1,0:T(8,128)(2,1)S(1)} all-reduce(f32[2,64,128]{2,1,0:T(8,128)S(1)} %pad_maximum_fusion.2), channel_id=1, replica_groups=mesh['lat'=16,'field'=2] {'lat','field'}, use_global_device_ids=true, to_apply=%region_0.1 | all-reduce | flops 16384 | bytes 98304 | tf_op jit(solution)/shard_map/psum | solution.py:71
  73.3 0.1 reshape.350
  73.4 0.1 reduce_sum.9
  73.5 0.1 div.10
  73.7 0.1 sub.26
  73.8 0.1 sub.27
  73.9 0.1 convert_element_type.92
  74.0 0.2 convert_element_type.86
  74.2 1.0 %fusion = bf16[1536,128]{1,0:T(8,128)(2,1)} fusion(bf16[1536,64]{1,0:T(8,128)(2,1)S(1)} %convert_element_type.86, bf16[128,64]{1,0:T(8,128)(2,1)S(1)} %convert_element_type.92), kind=kOutput, calls=%fused_computation.2 | convolution fusion | flops 25559040 | bytes 606208 | tf_op jit(solution)/shard_map/dot_general | solution.py:76
  (24 shorter events, 0.3 us)
Async XLA Ops:
  0.0 0.8 %copy-start.1 = (s32[16,8]{0,1:T(8,128)S(1)}, s32[16,8]{0,1:T(8,128)}, u32[]{:S(2)}) copy-start(s32[16,8]{0,1:T(8,128)} %param.6) | copy-start | bytes 1540
  15.4 9.5 %copy-start = (bf16[8,48,96]{2,1,0:T(8,128)(2,1)S(1)}, bf16[8,48,96]{2,1,0:T(8,128)(2,1)}, u32[]{:S(2)}) copy-start(bf16[8,48,96]{2,1,0:T(8,128)(2,1)} %param.5) | copy-start | bytes 221188
  15.4 17.1 %all-to-all-start = ((bf16[16,2,8,3,128]{4,2,3,1,0:T(8,128)(2,1)}), bf16[16,2,8,3,128]{4,2,3,1,0:T(8,128)(2,1)S(1)}, u32[]{:S(2)}, u32[]{:S(2)}) async-start(bf16[16,2,8,3,128]{4,2,3,1,0:T(8,128)(2,1)} %constant_dynamic-update-slice_fusion), calls=%async_computation | async-start | bytes 393216 | tf_op jit(solution)/shard_map/all_to_all | solution.py:46
  23.9 0.7 copy-start.2
